TPU v7x, 512 devices: a whole 4x8x8 slice. The times are simulated.
512 devices in a mesh: dp: 16 (over z, core), expert: 32 (over x, y).
Axes of the slice: x: 4, y: 8, z: 8, core: 2. Of those that a mesh axis runs over, the one named last changes fastest.
Arguments:
- pivot_states: bfloat16 [65536, 2048], P(('dp', 'expert')), may hold values from -6 to 6
- queries: bfloat16 [65536, 2048], P(('dp', 'expert')), may hold values from -8 to 8
- keys: bfloat16 [65536, 2048], P(('dp', 'expert')), may hold values from -8 to 8
- values: bfloat16 [65536, 2048], P(('dp', 'expert')), may hold values from -6 to 6
- pack_pos: int32 [65536], P(('dp', 'expert')), may hold values from 0 to 2047, as said below
- segment_ids: int32 [512, 128], P(('dp', 'expert')), may hold values from 0 to 7, never falling along the last dimension, each value on 1 to 64 neighbouring positions
- expert_ids: int32 [65536, 2], P(('dp', 'expert')), may hold values from 0 to 127, all different within a row
- gate_code: int32 [65536, 2], P(('dp', 'expert')), may hold values from 6554 to 65535
- ln_gain: float32 [2048], replicated, may hold values from 0.5 to 1.5
- ln_bias: float32 [2048], replicated, may hold values from -3 to 3
- w_in: bfloat16 [32, 2048, 4096], P('expert', None, 'dp'), may hold values from -0.125 to 0.125
- b_in: float32 [32, 4096], P('expert', 'dp'), may hold values from -3 to 3
- w_out: bfloat16 [32, 4096, 2048], P('expert', 'dp'), may hold values from -0.09375 to 0.09375
- b_out: float32 [32, 2048], replicated, may hold values from -3 to 3
Outputs:
- layer_out: bfloat16 [65536, 2048], P(('dp', 'expert'))
Inputs may be any that keep to these rules, and one draw needn't show every extreme that they name: Within one index of expert, pack_pos over the devices of dp is a permutation, and each device's tokens go exactly 8 to each packed block of its column. `expert_ids`: only ids below 32 belong to the experts of this round.
All inputs are finite; a program needn't handle non-finite values.
Results may differ from a plain program's by a relative error of at most 0.0055.
Values may be sent and summed in bfloat16 or wider, within the bound.
A program may use at most 64 MiB of HBM per device.

v0:
```python
import math
import jax
import jax.numpy as jnp
from jax import lax
from jax.sharding import PartitionSpec as P

HEAD_DIM = 128
ROUNDS = 4
epsilon = 1e-05
mask_fill = -1e30


def per_device(
    pivot_states,
    queries,
    keys,
    values,
    pack_pos,
    segment_ids,
    expert_ids,
    gate_code,
    ln_gain,
    ln_bias,
    w_in,
    b_in,
    w_out,
    b_out,
):
    tok_count = pivot_states.shape[0]
    model_width = pivot_states.shape[1]
    dp_count = lax.axis_size("dp")
    expert_count = lax.axis_size("expert")
    per_target = tok_count // dp_count
    target_block = pack_pos // tok_count
    offsets = pack_pos % tok_count
    target_hot = (target_block[:, None] == jnp.arange(dp_count, dtype=jnp.int32)[None, :]).astype(
        jnp.int32
    )
    bucket_rank = jnp.sum(jnp.cumsum(target_hot, axis=0) * target_hot, axis=1) - 1
    send_index = target_block * per_target + bucket_rank
    joined = jnp.concatenate([pivot_states, queries, keys, values], axis=1)
    send_rows = jnp.zeros_like(joined).at[send_index].set(joined)
    send_offsets = jnp.zeros_like(offsets).at[send_index].set(offsets)
    recv_rows, recv_offsets = (
        lax.all_to_all(send_rows, "dp", split_axis=0, concat_axis=0, tiled=True),
        lax.all_to_all(send_offsets, "dp", split_axis=0, concat_axis=0, tiled=True),
    )
    packed = jnp.zeros_like(recv_rows).at[recv_offsets].set(recv_rows)
    state_rows = packed[:, :model_width]
    query_rows = packed[:, model_width : 2 * model_width]
    key_rows = packed[:, 2 * model_width : 3 * model_width]
    value_rows = packed[:, 3 * model_width :]
    head_count = model_width // HEAD_DIM
    key_heads = key_rows.reshape(tok_count, head_count, HEAD_DIM)
    value_heads = value_rows.reshape(tok_count, head_count, HEAD_DIM)
    seg_row = segment_ids[0]
    block_rows = min(tok_count, 512)
    block_count = tok_count // block_rows
    score_scale = 1.0 / math.sqrt(HEAD_DIM)

    def attend(block_args):
        query_block, seg_block = block_args
        query_heads = query_block.reshape(block_rows, head_count, HEAD_DIM)
        scores = (
            jnp.einsum("qhd,khd->hqk", query_heads, key_heads, preferred_element_type=jnp.float32)
            * score_scale
        )
        same_doc = seg_block[:, None] == seg_row[None, :]
        scores = jnp.where(same_doc[None, :, :], scores, mask_fill)
        top_score = jnp.max(scores, axis=2, keepdims=True)
        exp_terms = jnp.exp(scores - top_score)
        softmax_weights = (exp_terms / jnp.sum(exp_terms, axis=2, keepdims=True)).astype(
            jnp.bfloat16
        )
        mixed_heads = jnp.einsum(
            "hqk,khd->qhd", softmax_weights, value_heads, preferred_element_type=jnp.float32
        )
        return mixed_heads.reshape(block_rows, model_width)

    attended = lax.map(
        attend,
        (
            query_rows.reshape(block_count, block_rows, model_width),
            seg_row.reshape(block_count, block_rows),
        ),
    )
    hidden_state = state_rows.astype(jnp.float32) + attended.reshape(tok_count, model_width)
    mean_value = jnp.mean(hidden_state, axis=1, keepdims=True)
    centered = hidden_state - mean_value
    variance = jnp.mean(centered * centered, axis=1, keepdims=True)
    normed = (centered * lax.rsqrt(variance + epsilon) * ln_gain + ln_bias).astype(jnp.bfloat16)
    capacity = max(2, 2 * tok_count // (ROUNDS * expert_count))
    assigned = jnp.concatenate([expert_ids[:, 0], expert_ids[:, 1]])
    expert_hot = (assigned[:, None] == jnp.arange(expert_count, dtype=jnp.int32)[None, :]).astype(
        jnp.int32
    )
    slot_rank = jnp.sum(jnp.cumsum(expert_hot, axis=0) * expert_hot, axis=1) - 1
    kept_mask = (assigned < expert_count) & (slot_rank < capacity)
    overflow = expert_count * capacity
    slot_index = jnp.where(kept_mask, assigned * capacity + slot_rank, overflow)
    buffer = jnp.zeros((overflow, model_width), jnp.bfloat16)
    buffer = (
        buffer.at[slot_index[:tok_count]]
        .set(normed, mode="drop")
        .at[slot_index[tok_count:]]
        .set(normed, mode="drop")
    )
    first_matrix = w_in[0]
    bias_in_row = b_in[0]
    second_matrix = w_out[0]
    arrived = lax.all_to_all(
        buffer.reshape(expert_count, capacity, model_width),
        "expert",
        split_axis=0,
        concat_axis=0,
        tiled=True,
    )
    arrived = arrived.reshape(overflow, model_width)
    hidden = jnp.dot(
        lax.all_gather(arrived, "dp", axis=0, tiled=True),
        first_matrix,
        preferred_element_type=jnp.float32,
    )
    hidden = jnp.maximum(hidden + bias_in_row, 0.0).astype(jnp.bfloat16)
    partial_value = jnp.dot(hidden, second_matrix, preferred_element_type=jnp.float32).astype(
        jnp.bfloat16
    )
    summed = lax.psum(partial_value, "dp").astype(jnp.float32)
    summed = lax.dynamic_slice_in_dim(summed, lax.axis_index("dp") * overflow, overflow, 0)
    bias_out_row = lax.dynamic_slice_in_dim(b_out, lax.axis_index("expert"), 1, 0)
    results = (summed + bias_out_row).astype(jnp.bfloat16)
    returned = lax.all_to_all(
        results.reshape(expert_count, capacity, model_width),
        "expert",
        split_axis=0,
        concat_axis=0,
        tiled=True,
    )
    returned = returned.reshape(overflow, model_width)
    gate_values = gate_code.astype(jnp.float32) / 65536.0
    gate_flat = jnp.concatenate([gate_values[:, 0], gate_values[:, 1]])
    weights = jnp.where(kept_mask, gate_flat, 0.0)
    guard_index = jnp.minimum(slot_index, overflow - 1)
    picked = returned[guard_index].astype(jnp.float32) * weights[:, None]
    layer_out = hidden_state + picked[:tok_count] + picked[tok_count:]
    return layer_out.astype(jnp.bfloat16)


def solution(mesh):
    return jax.shard_map(
        per_device,
        mesh=mesh,
        in_specs=(
            P(("dp", "expert"), None),
            P(("dp", "expert"), None),
            P(("dp", "expert"), None),
            P(("dp", "expert"), None),
            P(("dp", "expert")),
            P(("dp", "expert"), None),
            P(("dp", "expert"), None),
            P(("dp", "expert"), None),
            P(),
            P(),
            P("expert", None, "dp"),
            P("expert", "dp"),
            P("expert", "dp", None),
            P(),
        ),
        out_specs=P(("dp", "expert"), None),
        check_vma=False,
    )
```

profile of v0, /device:TPU:8, one launch (start us, length us, event | category | flops | bytes accessed | tf_op | source)
XLA Modules:
  0.0 335.2 jit_solution(7050097430861302124)
XLA Ops:
  6.5 0.8 and_select_fusion.1
  7.3 0.1 fusion.28
  7.4 0.2 reduce_window_sum.26
  7.6 0.2 select_reduce_fusion
  7.7 1.0 scatter_custom_fusion
  8.7 0.7 all_to_all.22
  9.4 10.4 %all-to-all-start = ((s32[16,8,1]{1,2,0:T(1,128)}), s32[16,8,1]{1,2,0:T(1,128)S(1)}, u32[]{:S(2)}, u32[]{:S(2)}) async-start(s32[16,8,1]{1,2,0:T(1,128)} %bitcast), calls=%async_computation | async-start | bytes 16384 | tf_op jit(solution)/shard_map/all_to_all | solution.py:46
  19.8 6.0 %scatter_custom_fusion.1 = bf16[128,8192]{1,0:T(8,128)(2,1)} fusion(s32[128]{0:T(128)S(1)} %compare_select_fusion.4, bf16[128,2048]{1,0:T(8,128)(2,1)} %param.17, bf16[]{:T(256)} %constant.122, bf16[128,2048]{1,0:T(8,128)(2,1)} %param.16, bf16[128,2048]{1,0:T(8,128)(2,1)} %param.15, bf16[128,2048]{1,0:T(8,128)(2,1)} %param.14, bf16[]{:T(256)} %constant.46.clone.1), kind=kCustom, calls=%fused_computation.8 | custom fusion | flops 8388608 | bytes 4194308 | tf_op jit(solution)/shard_map/scatter | solution.py:42
  25.8 1.6 all-to-all-done
  27.4 5.8 %all-to-all-start.1 = ((bf16[16,8,8192]{2,1,0:T(8,128)(2,1)}), bf16[16,8,8192]{2,1,0:T(8,128)(2,1)}, u32[]{:S(2)}, u32[]{:S(2)}) async-start(bf16[16,8,8192]{2,1,0:T(8,128)(2,1)} %bitcast.2), calls=%async_computation.1 | async-start | bytes 4194304 | tf_op jit(solution)/shard_map/all_to_all | solution.py:45
  33.3 0.6 reduce-window.6
  33.9 0.2 slice_reduce_fusion
  34.1 0.1 fusion.30
  34.3 0.1 broadcast_compare_fusion
  34.4 0.5 broadcast.249
  34.9 0.7 reduce.5
  35.6 0.1 all_to_all.24
  35.7 46.8 %all-to-all-done.1 = bf16[16,8,8192]{2,1,0:T(8,128)(2,1)} async-done(((bf16[16,8,8192]{2,1,0:T(8,128)(2,1)}), bf16[16,8,8192]{2,1,0:T(8,128)(2,1)}, u32[]{:S(2)}, u32[]{:S(2)}) %all-to-all-start.1) | async-done | bytes 2097184 | tf_op jit(solution)/shard_map/all_to_all | solution.py:45
  82.5 5.2 %scatter_custom_fusion.2 = bf16[128,8192]{1,0:T(8,128)(2,1)S(1)} fusion(s32[128]{0:T(128)S(1)} %fusion.32, bf16[16,8,8192]{2,1,0:T(8,128)(2,1)} %all-to-all-done.1, bf16[]{:T(256)} %constant.46.clone.1), kind=kCustom, calls=%fused_computation.16 | custom fusion | bytes 4194306 | tf_op jit(solution)/shard_map/scatter | solution.py:48
  87.7 1.3 fusion.39
  89.0 2.1 copy.28
  91.0 1.4 copy.29
  92.4 1.4 fusion.13
  93.8 0.2 fusion.41
  94.1 0.3 copy.27
  94.3 1.4 fusion.22
  95.8 1.6 copy.33
  97.3 1.2 fusion.38
  98.6 1.3 multiply_reduce_fusion
  99.9 1.3 add_convert_fusion
  101.2 1.4 scatter_custom_fusion.3
  102.6 1.5 scatter_fusion
  104.1 0.2 reshape.242
  104.3 22.6 %all_to_all.34 = bf16[32,2,2048]{2,1,0:T(2,128)(2,1)S(1)} all-to-all(bf16[32,2,2048]{2,1,0:T(2,128)(2,1)S(1)} %reshape.242), channel_id=1, replica_groups=mesh['dp'=16,'expert'=32] {'expert'}, dimensions={0} | all-to-all | bytes 524288 | tf_op jit(solution)/shard_map/all_to_all | solution.py:111
  126.9 0.8 reshape.243
  127.8 38.2 %all-gather.2.cloned.1.call-done = bf16[1024,2048]{1,0:T(8,128)(2,1)} async-done(((bf16[64,2048]{1,0:T(8,128)(2,1)}), bf16[1024,2048]{1,0:T(8,128)(2,1)}) %all-gather.2.cloned.1.call-update) | async-done | bytes 4194320 | tf_op jit(solution)/shard_map/all_gather | solution.py:120
  166.0 8.8 %convolution_convert_fusion = bf16[1024,2048]{1,0:T(8,128)(2,1)} fusion(bf16[1024,2048]{1,0:T(8,128)(2,1)} %all-gather.2.cloned.1.call-done, bf16[1,256,2048]{2,1,0:T(8,128)(2,1)S(1)} %copy-done, bf16[1,2048,256]{2,1,0:T(8,128)(2,1)} %param.24, f32[256]{0:T(256)S(1)} %bitcast.65), kind=kOutput, calls=%fused_computation.7 | convolution fusion | flops 2150367232 | bytes 10486784 | tf_op jit(solution)/shard_map/dot_general | solution.py:125
  174.8 0.6 copy-done.7
  175.5 0.9 constant_dynamic-slice_fusion
  176.3 124.8 %all-reduce.2.cloned.1.call-done = bf16[1024,2048]{1,0:T(8,128)(2,1)} async-done(((bf16[1024,2048]{1,0:T(8,128)(2,1)}), bf16[1024,2048]{1,0:T(8,128)(2,1)}) %all-reduce.2.cloned.1.call-update) | async-done | bytes 4194320 | tf_op jit(solution)/shard_map/psum | solution.py:128
  301.2 1.0 add_convert_fusion.1
  302.2 0.9 reshape.244
  303.0 9.8 %all-to-all-start.3 = ((bf16[32,2,2048]{2,1,0:T(2,128)(2,1)}), bf16[32,2,2048]{2,1,0:T(2,128)(2,1)S(1)}, u32[]{:S(2)}, u32[]{:S(2)}) async-start(bf16[32,2,2048]{2,1,0:T(2,128)(2,1)} %reshape.244), calls=%async_computation.3 | async-start | bytes 524288 | tf_op jit(solution)/shard_map/all_to_all | solution.py:132
  312.9 11.5 %all-to-all-done.3 = bf16[32,2,2048]{2,1,0:T(2,128)(2,1)S(1)} async-done(((bf16[32,2,2048]{2,1,0:T(2,128)(2,1)}), bf16[32,2,2048]{2,1,0:T(2,128)(2,1)S(1)}, u32[]{:S(2)}, u32[]{:S(2)}) %all-to-all-start.3) | async-done | bytes 262176 | tf_op jit(solution)/shard_map/all_to_all | solution.py:132
  324.5 0.1 reshape.245
  324.6 1.4 gather_fusion
  325.9 0.2 convert_multiply_fusion
  326.1 2.2 fusion.16
  (37 shorter events, 0.3 us)
Async XLA Ops:
  6.5 159.5 %copy-start = (bf16[1,256,2048]{2,1,0:T(8,128)(2,1)S(1)}, bf16[1,256,2048]{2,1,0:T(8,128)(2,1)}, u32[]{:S(2)}) copy-start(bf16[1,256,2048]{2,1,0:T(8,128)(2,1)} %param.26) | copy-start | bytes 3145732
  9.4 18.0 %all-to-all-start = ((s32[16,8,1]{1,2,0:T(1,128)}), s32[16,8,1]{1,2,0:T(1,128)S(1)}, u32[]{:S(2)}, u32[]{:S(2)}) async-start(s32[16,8,1]{1,2,0:T(1,128)} %bitcast), calls=%async_computation | async-start | bytes 16384 | tf_op jit(solution)/shard_map/all_to_all | solution.py:46
  27.4 5.9 %copy-start.6 = (s32[128,2]{0,1:T(2,128)S(1)}, s32[128,2]{0,1:T(2,128)}, u32[]{:S(2)}) copy-start(s32[128,2]{0,1:T(2,128)} %param.20) | copy-start | bytes 3076
  27.4 6.9 %copy-start.5 = (s32[1,128]{1,0:T(1,128)S(1)}, s32[1,128]{1,0:T(1,128)}, u32[]{:S(2)}) copy-start(s32[1,128]{1,0:T(1,128)} %param.19) | copy-start | bytes 1540
  27.4 55.1 %all-to-all-start.1 = ((bf16[16,8,8192]{2,1,0:T(8,128)(2,1)}), bf16[16,8,8192]{2,1,0:T(8,128)(2,1)}, u32[]{:S(2)}, u32[]{:S(2)}) async-start(bf16[16,8,8192]{2,1,0:T(8,128)(2,1)} %bitcast.2), calls=%async_computation.1 | async-start | bytes 4194304 | tf_op jit(solution)/shard_map/all_to_all | solution.py:45
  33.2 132.8 %all-gather.2.cloned.1.call-start = ((), (), s32[]{:S(2)}) async-start(), calls=%async_computation.4 | async-start | bytes 4456448 | tf_op jit(solution)/shard_map/all_gather | solution.py:120
  87.7 3.3 copy-start.1
  91.0 3.0 copy-start.2
  97.3 2.6 copy-start.3
  97.3 2.6 copy-start.4
  102.6 63.4 %copy-start.8 = (f32[1,256]{1,0:T(1,128)S(1)}, f32[1,256]{1,0:T(1,128)}, u32[]{:S(2)}) copy-start(f32[1,256]{1,0:T(1,128)} %param.25) | copy-start | bytes 3076
  127.8 173.4 %all-reduce.2.cloned.1.call-start = ((), (), s32[]{:S(2)}) async-start(), calls=%async_computation.5 | async-start | bytes 8388608 | tf_op jit(solution)/shard_map/psum | solution.py:128
  174.8 0.7 copy-start.7
  303.0 21.4 %all-to-all-start.3 = ((bf16[32,2,2048]{2,1,0:T(2,128)(2,1)}), bf16[32,2,2048]{2,1,0:T(2,128)(2,1)S(1)}, u32[]{:S(2)}, u32[]{:S(2)}) async-start(bf16[32,2,2048]{2,1,0:T(2,128)(2,1)} %reshape.244), calls=%async_computation.3 | async-start | bytes 524288 | tf_op jit(solution)/shard_map/all_to_all | solution.py:132
Sparse Core Ops, SparseCore 0:
  127.9 38.0 all-gather.1
  174.9 126.1 all-reduce.1
where the time goes:
time: 336 us; the launch traced here: 335 us
  waiting for transfers between devices  223 us (66%)
  starting transfers between devices  26.2 us (8%)
  blocking collectives  22.6 us (7%)
  local copies, waits for them, and re-layouts  21.9 us (7%)
  other arithmetic  16.2 us (5%)
  between operations  13.7 us (4%)
  matrix products  11.6 us (3%)
    psum x1, waiting for transfers between devices, per_device(): summed = lax.psum(partial_value, 'dp').astype(jnp.float32)  125 us
    all_to_all x1, waiting for transfers between devices, per_device(): lax.all_to_all(send_rows, 'dp', split_axis=0, concat_axis=0, tiled=True)  46.8 us
    all_gather x1, waiting for transfers between devices, per_device(): lax.all_gather(arrived, 'dp', axis=0, tiled=True)  38.2 us
    all_to_all x1, blocking collectives, per_device(): lax.all_to_all(buffer.reshape(expert_count, capacity, model_width), 'expe...  22.6 us
    all_to_all x1, waiting for transfers between devices, per_device(): lax.all_to_all(results.reshape(expert_count, capacity, model_width), 'exp...  11.5 us
    all_to_all x1, starting transfers between devices, per_device(): lax.all_to_all(send_offsets, 'dp', split_axis=0, concat_axis=0, tiled=True)  10.4 us
    all_to_all x1, starting transfers between devices, per_device(): lax.all_to_all(results.reshape(expert_count, capacity, model_width), 'exp...  9.85 us
    dot_general x1, matrix products, per_device(): jnp.dot(hidden, second_matrix, preferred_element_type=jnp.float32)  8.76 us
  transfers between devices with their start and end apart: 5, of which 5 were waited for; matrix products, arithmetic and copies ran while one was open for 3% of the time, Pallas kernels for 0%

commit v1 on v0

--- a/solution.py
+++ b/solution.py
@@ -117,7 +117,15 @@
     )
     arrived = arrived.reshape(overflow, model_width)
     hidden = jnp.dot(
-        lax.all_gather(arrived, "dp", axis=0, tiled=True),
+        jnp.concatenate(
+            jax.lax.all_to_all(
+                jnp.stack(jax.lax.axis_size("dp") * [arrived], 0),
+                axis_name="dp",
+                split_axis=0,
+                concat_axis=0,
+            ),
+            0,
+        ),
         first_matrix,
         preferred_element_type=jnp.float32,
     )

time: 336 us -> 391 us (1.16)
  blocking collectives: 22.6 us -> 122 us
  waiting for transfers between devices: 223 us -> 179 us
    all_to_all x0 -> x1, blocking collectives: none -> 99.2 us  [per_device(): jax.lax.all_to_all(jnp.stack(jax.lax.axis_size('dp') * [arrived], 0), axi...]
    all_gather x1 -> x0, waiting for transfers between devices: 38.2 us -> none  [per_device(): lax.all_gather(arrived, 'dp', axis=0, tiled=True)]
    psum x1, waiting for transfers between devices: 125 us -> 119 us  [per_device(): summed = lax.psum(partial_value, 'dp').astype(jnp.float32)]
  transfers between devices with their start and end apart: 5 -> 4, of which waited for: 5 -> 4; matrix products, arithmetic and copies ran while one was open for 3% -> 2% of each run, Pallas kernels for 0% -> 0%
where the time goes in v1:
time: 391 us; the launch traced here: 390 us
  waiting for transfers between devices  179 us (46%)
  blocking collectives  122 us (31%)
  starting transfers between devices  26.1 us (7%)
  local copies, waits for them, and re-layouts  21.7 us (6%)
  other arithmetic  16.2 us (4%)
  between operations  13.7 us (4%)
  matrix products  11.3 us (3%)
    psum x1, waiting for transfers between devices, per_device(): summed = lax.psum(partial_value, 'dp').astype(jnp.float32)  119 us
    all_to_all x1, blocking collectives, per_device(): jax.lax.all_to_all(jnp.stack(jax.lax.axis_size('dp') * [arrived], 0), axi...  99.2 us
    all_to_all x1, waiting for transfers between devices, per_device(): lax.all_to_all(send_rows, 'dp', split_axis=0, concat_axis=0, tiled=True)  46.8 us
    all_to_all x1, blocking collectives, per_device(): lax.all_to_all(buffer.reshape(expert_count, capacity, model_width), 'expe...  22.6 us
    all_to_all x1, waiting for transfers between devices, per_device(): lax.all_to_all(results.reshape(expert_count, capacity, model_width), 'exp...  11.5 us
    all_to_all x1, starting transfers between devices, per_device(): lax.all_to_all(send_offsets, 'dp', split_axis=0, concat_axis=0, tiled=True)  10.4 us
    all_to_all x1, starting transfers between devices, per_device(): lax.all_to_all(results.reshape(expert_count, capacity, model_width), 'exp...  9.85 us
    dot_general x1, matrix products, per_device(): jnp.dot(hidden, second_matrix, preferred_element_type=jnp.float32)  8.46 us
  transfers between devices with their start and end apart: 4, of which 4 were waited for; matrix products, arithmetic and copies ran while one was open for 2% of the time, Pallas kernels for 0%

profile of v1, /device:TPU:8, one launch (start us, length us, event | category | flops | bytes accessed | tf_op | source)
XLA Modules:
  0.0 390.2 jit_solution(15437623915543173398)
XLA Ops:
  6.5 0.8 and_select_fusion.1
  7.4 0.2 reduce_window_sum.26
  7.6 0.2 select_reduce_fusion
  7.7 1.0 scatter_custom_fusion
  8.7 0.7 all_to_all.25
  9.4 10.4 %all-to-all-start = ((s32[16,8,1]{1,2,0:T(1,128)}), s32[16,8,1]{1,2,0:T(1,128)S(1)}, u32[]{:S(2)}, u32[]{:S(2)}) async-start(s32[16,8,1]{1,2,0:T(1,128)} %bitcast), calls=%async_computation | async-start | bytes 16384 | tf_op jit(solution)/shard_map/all_to_all | solution.py:46
  19.8 6.0 %scatter_custom_fusion.1 = bf16[128,8192]{1,0:T(8,128)(2,1)} fusion(s32[128]{0:T(128)S(1)} %compare_select_fusion.4, bf16[128,2048]{1,0:T(8,128)(2,1)} %param.17, bf16[]{:T(256)} %constant.122, bf16[128,2048]{1,0:T(8,128)(2,1)} %param.16, bf16[128,2048]{1,0:T(8,128)(2,1)} %param.15, bf16[128,2048]{1,0:T(8,128)(2,1)} %param.14, bf16[]{:T(256)} %constant.46.clone.1), kind=kCustom, calls=%fused_computation.8 | custom fusion | flops 8388608 | bytes 4194308 | tf_op jit(solution)/shard_map/scatter | solution.py:42
  25.8 1.6 all-to-all-done
  27.4 5.8 %all-to-all-start.1 = ((bf16[16,8,8192]{2,1,0:T(8,128)(2,1)}), bf16[16,8,8192]{2,1,0:T(8,128)(2,1)}, u32[]{:S(2)}, u32[]{:S(2)}) async-start(bf16[16,8,8192]{2,1,0:T(8,128)(2,1)} %bitcast.2), calls=%async_computation.1 | async-start | bytes 4194304 | tf_op jit(solution)/shard_map/all_to_all | solution.py:45
  33.3 0.6 reduce-window.6
  33.9 0.2 slice_reduce_fusion
  34.1 0.1 fusion.30
  34.3 0.1 broadcast_compare_fusion
  34.4 0.5 broadcast.250
  34.9 0.7 reduce.5
  35.6 0.1 all_to_all.27
  35.7 46.8 %all-to-all-done.1 = bf16[16,8,8192]{2,1,0:T(8,128)(2,1)} async-done(((bf16[16,8,8192]{2,1,0:T(8,128)(2,1)}), bf16[16,8,8192]{2,1,0:T(8,128)(2,1)}, u32[]{:S(2)}, u32[]{:S(2)}) %all-to-all-start.1) | async-done | bytes 2097184 | tf_op jit(solution)/shard_map/all_to_all | solution.py:45
  82.5 5.2 %scatter_custom_fusion.2 = bf16[128,8192]{1,0:T(8,128)(2,1)S(1)} fusion(s32[128]{0:T(128)S(1)} %fusion.32, bf16[16,8,8192]{2,1,0:T(8,128)(2,1)} %all-to-all-done.1, bf16[]{:T(256)} %constant.46.clone.1), kind=kCustom, calls=%fused_computation.16 | custom fusion | bytes 4194306 | tf_op jit(solution)/shard_map/scatter | solution.py:48
  87.7 1.3 fusion.39
  89.0 2.1 copy.28
  91.0 1.4 copy.29
  92.4 1.4 fusion.13
  93.8 0.2 fusion.41
  94.1 0.3 copy.27
  94.3 1.4 fusion.22
  95.8 1.6 copy.33
  97.3 1.2 fusion.38
  98.6 1.3 multiply_reduce_fusion
  99.9 1.3 add_convert_fusion
  101.2 1.4 scatter_custom_fusion.3
  102.6 1.5 scatter_fusion
  104.1 0.2 reshape.244
  104.3 22.6 %all_to_all.39 = bf16[32,2,2048]{2,1,0:T(2,128)(2,1)S(1)} all-to-all(bf16[32,2,2048]{2,1,0:T(2,128)(2,1)S(1)} %reshape.244), channel_id=1, replica_groups=mesh['dp'=16,'expert'=32] {'expert'}, dimensions={0} | all-to-all | bytes 524288 | tf_op jit(solution)/shard_map/all_to_all | solution.py:111
  126.9 0.1 stack_reshape.2
  127.0 0.5 stack.3
  127.6 99.2 %all_to_all.40 = bf16[16,64,2048]{2,1,0:T(8,128)(2,1)} all-to-all(bf16[16,64,2048]{2,1,0:T(8,128)(2,1)S(1)} %stack.3), channel_id=1, replica_groups=mesh['dp'=16,'expert'=32] {'dp'}, dimensions={0} | all-to-all | bytes 8388608 | tf_op jit(solution)/shard_map/all_to_all | solution.py:121
  226.8 8.5 %convolution_convert_fusion = bf16[1024,2048]{1,0:T(8,128)(2,1)} fusion(bf16[1024,2048]{1,0:T(8,128)(2,1)} %bitcast.58, bf16[1,256,2048]{2,1,0:T(8,128)(2,1)S(1)} %copy-done, bf16[1,2048,256]{2,1,0:T(8,128)(2,1)S(1)} %copy-done.8, f32[256]{0:T(256)S(1)} %bitcast.67), kind=kOutput, calls=%fused_computation.7 | convolution fusion | flops 2150367232 | bytes 10486784 | tf_op jit(solution)/shard_map/dot_general | solution.py:133
  235.2 0.6 copy-done.7
  235.9 0.9 constant_dynamic-slice_fusion
  236.8 119.4 %all-reduce.2.cloned.1.call-done = bf16[1024,2048]{1,0:T(8,128)(2,1)} async-done(((bf16[1024,2048]{1,0:T(8,128)(2,1)}), bf16[1024,2048]{1,0:T(8,128)(2,1)}) %all-reduce.2.cloned.1.call-update) | async-done | bytes 4194320 | tf_op jit(solution)/shard_map/psum | solution.py:136
  356.2 1.0 add_convert_fusion.1
  357.2 0.9 reshape.246
  358.1 9.8 %all-to-all-start.4 = ((bf16[32,2,2048]{2,1,0:T(2,128)(2,1)}), bf16[32,2,2048]{2,1,0:T(2,128)(2,1)S(1)}, u32[]{:S(2)}, u32[]{:S(2)}) async-start(bf16[32,2,2048]{2,1,0:T(2,128)(2,1)} %reshape.246), calls=%async_computation.4 | async-start | bytes 524288 | tf_op jit(solution)/shard_map/all_to_all | solution.py:140
  368.0 11.5 %all-to-all-done.4 = bf16[32,2,2048]{2,1,0:T(2,128)(2,1)S(1)} async-done(((bf16[32,2,2048]{2,1,0:T(2,128)(2,1)}), bf16[32,2,2048]{2,1,0:T(2,128)(2,1)S(1)}, u32[]{:S(2)}, u32[]{:S(2)}) %all-to-all-start.4) | async-done | bytes 262176 | tf_op jit(solution)/shard_map/all_to_all | solution.py:140
  379.5 0.1 reshape.247
  379.6 1.4 gather_fusion
  381.0 0.2 convert_multiply_fusion
  381.2 2.2 fusion.16
  (38 shorter events, 0.3 us)
Async XLA Ops:
  6.5 220.2 %copy-start = (bf16[1,256,2048]{2,1,0:T(8,128)(2,1)S(1)}, bf16[1,256,2048]{2,1,0:T(8,128)(2,1)}, u32[]{:S(2)}) copy-start(bf16[1,256,2048]{2,1,0:T(8,128)(2,1)} %param.26) | copy-start | bytes 3145732
  9.4 18.0 %all-to-all-start = ((s32[16,8,1]{1,2,0:T(1,128)}), s32[16,8,1]{1,2,0:T(1,128)S(1)}, u32[]{:S(2)}, u32[]{:S(2)}) async-start(s32[16,8,1]{1,2,0:T(1,128)} %bitcast), calls=%async_computation | async-start | bytes 16384 | tf_op jit(solution)/shard_map/all_to_all | solution.py:46
  27.4 5.9 %copy-start.6 = (s32[128,2]{0,1:T(2,128)S(1)}, s32[128,2]{0,1:T(2,128)}, u32[]{:S(2)}) copy-start(s32[128,2]{0,1:T(2,128)} %param.20) | copy-start | bytes 3076
  27.4 6.9 %copy-start.5 = (s32[1,128]{1,0:T(1,128)S(1)}, s32[1,128]{1,0:T(1,128)}, u32[]{:S(2)}) copy-start(s32[1,128]{1,0:T(1,128)} %param.19) | copy-start | bytes 1540
  27.4 55.1 %all-to-all-start.1 = ((bf16[16,8,8192]{2,1,0:T(8,128)(2,1)}), bf16[16,8,8192]{2,1,0:T(8,128)(2,1)}, u32[]{:S(2)}, u32[]{:S(2)}) async-start(bf16[16,8,8192]{2,1,0:T(8,128)(2,1)} %bitcast.2), calls=%async_computation.1 | async-start | bytes 4194304 | tf_op jit(solution)/shard_map/all_to_all | solution.py:45
  33.2 322.9 %all-reduce.2.cloned.1.call-start = ((), (), s32[]{:S(2)}) async-start(), calls=%async_computation.5 | async-start | bytes 8388608 | tf_op jit(solution)/shard_map/psum | solution.py:136
  87.7 3.3 copy-start.1
  91.0 3.0 copy-start.2
  97.3 2.6 copy-start.3
  97.3 2.6 copy-start.4
  127.6 99.2 %copy-start.8 = (bf16[1,2048,256]{2,1,0:T(8,128)(2,1)S(1)}, bf16[1,2048,256]{2,1,0:T(8,128)(2,1)}, u32[]{:S(2)}) copy-start(bf16[1,2048,256]{2,1,0:T(8,128)(2,1)} %param.24) | copy-start | bytes 3145732
  127.6 99.2 %copy-start.9 = (f32[1,256]{1,0:T(1,128)S(1)}, f32[1,256]{1,0:T(1,128)}, u32[]{:S(2)}) copy-start(f32[1,256]{1,0:T(1,128)} %param.25) | copy-start | bytes 3076
  235.2 0.7 copy-start.7
  358.1 21.4 %all-to-all-start.4 = ((bf16[32,2,2048]{2,1,0:T(2,128)(2,1)}), bf16[32,2,2048]{2,1,0:T(2,128)(2,1)S(1)}, u32[]{:S(2)}, u32[]{:S(2)}) async-start(bf16[32,2,2048]{2,1,0:T(2,128)(2,1)} %reshape.246), calls=%async_computation.4 | async-start | bytes 524288 | tf_op jit(solution)/shard_map/all_to_all | solution.py:140
Sparse Core Ops, SparseCore 0:
  235.4 120.7 all-reduce.1
